TPU v7x, 32 devices: a whole 2x2x4 slice. The times are simulated.
32 devices in a mesh: parts: 2 (over y), tm: 4 (over z), axial: 2 (over x), chan: 2 (over core).
Axes of the slice: x: 2, y: 2, z: 4, core: 2. Of those that a mesh axis runs over, the one named last changes fastest.
Arguments:
- frames_in: bfloat16 [48, 8, 64, 128], P(('parts', 'tm'), 'axial'), parts along dimension 0, may hold values from -6 to 6
- spatial_weight: bfloat16 [6, 3, 64, 144], P('parts', None, None, 'chan'), parts along dimension 0, may hold values from -0.25 to 0.25
- temporal_weight: bfloat16 [6, 144, 64], P('parts', 'chan'), parts along dimension 0, may hold values from -0.3125 to 0.3125
- upstream: bfloat16 [48, 8, 64, 128], P(('parts', 'tm'), 'axial'), parts along dimension 0, may hold values from -6 to 6
Outputs:
- output: bfloat16 [48, 8, 64, 128], P(('parts', 'tm'), 'axial', 'chan'), parts along dimension 0
- input_grad: bfloat16 [48, 8, 64, 128], P(('parts', 'tm'), 'axial', 'chan'), parts along dimension 0
- spatial_grad: float32 [6, 3, 64, 144], P('parts', None, None, 'chan'), parts along dimension 0
- temporal_grad: float32 [6, 144, 64], P('parts', 'chan'), parts along dimension 0
There are 2 independent parts, one for each index of `parts`. A program takes and returns all parts, laid end to end along the dimension named above; each array names one. Nothing has to cross between parts.
All inputs are finite; a program needn't handle non-finite values.
Results may differ from a plain program's by a relative error of at most 0.009.
Values may be sent and summed in bfloat16 or wider, within the bound.
A program may use at most 64 MiB of HBM per device.

v0:
```python
import math
import jax
import jax.numpy as jnp
from jax import lax
from jax.sharding import PartitionSpec as P


def extended_2(block, sides, width, periodic):
    for axis, dim in sides:
        count = lax.axis_size(axis)
        forward = [(i, i + 1) for i in range(count - 1)]
        if periodic:
            forward.append((count - 1, 0))
        backward = [(target, source) for source, target in forward]
        low = lax.ppermute(
            lax.slice_in_dim(block, block.shape[dim] - width, None, axis=dim), axis, forward
        )
        high = lax.ppermute(lax.slice_in_dim(block, 0, width, axis=dim), axis, backward)
        block = jnp.concatenate([low, block, high], axis=dim)
    return block


def spatial_conv(padded_rows, kernel):
    return lax.conv_general_dilated(
        padded_rows,
        kernel,
        (1, 1),
        ((0, 0), (1, 1)),
        dimension_numbers=("NHCW", "HWIO", "NHCW"),
        preferred_element_type=jnp.float32,
    )


def temporal_conv(hidden_wide, weight):
    frame_count = hidden_wide.shape[0] - 2
    summed = None
    for offset in range(3):
        contrib = jnp.einsum(
            "fhmw,mc->fhcw",
            hidden_wide[offset : offset + frame_count],
            weight[offset],
            preferred_element_type=jnp.float32,
        )
        summed = contrib if summed is None else summed + contrib
    return summed


def shards(frames_in, spatial_weight, temporal_weight, upstream):
    frame_dev, row_dev, channels, width_dev = frames_in.shape
    mid_share = temporal_weight.shape[1]
    axial_count = lax.axis_size("axial")
    core_count = lax.axis_size("chan")
    factor = 1.0 / math.sqrt(frame_dev * lax.axis_size("tm") * row_dev * axial_count * width_dev)
    spatial_kernel, temporal_kernel = (
        lax.all_gather(spatial_weight, "chan", axis=3, tiled=True),
        lax.all_gather(temporal_weight, "chan", axis=1, tiled=True),
    )
    mid_local = temporal_kernel.shape[1]
    frame_local = frame_dev // core_count
    first_frame = lax.axis_index("chan") * frame_local
    own_frames = lax.dynamic_slice_in_dim(frames_in, first_frame, frame_local, 0)
    upstream_local = lax.dynamic_slice_in_dim(upstream, first_frame, frame_local, 0)
    input_rows = extended_2(own_frames, (("axial", 1),), 1, False)
    preact = spatial_conv(input_rows, spatial_kernel)
    hidden = jax.nn.silu(preact).astype(jnp.bfloat16)
    stacked = jnp.concatenate([hidden, upstream_local], axis=2)
    extended = extended_2(stacked, ((("tm", "chan"), 0),), 1, True)
    hidden_wide = extended[:, :, :mid_local]
    upstream_wide = extended[:, :, mid_local:]
    output_full = temporal_conv(hidden_wide, temporal_kernel).astype(jnp.bfloat16)
    temporal_grad = factor * jnp.stack(
        [
            jnp.einsum(
                "fhmw,fhcw->mc",
                hidden_wide[offset : offset + frame_local],
                upstream_local,
                preferred_element_type=jnp.float32,
            )
            for offset in range(3)
        ]
    )
    grad_act = None
    for offset in range(3):
        contrib = jnp.einsum(
            "fhcw,mc->fhmw",
            upstream_wide[2 - offset : 2 - offset + frame_local],
            temporal_kernel[offset],
            preferred_element_type=jnp.float32,
        )
        grad_act = contrib if grad_act is None else grad_act + contrib
    sigma = jax.nn.sigmoid(preact)
    grad_pre = (grad_act * sigma * (1.0 + preact * (1.0 - sigma))).astype(jnp.bfloat16)
    grad_padded = extended_2(grad_pre, (("axial", 1),), 1, False)
    input_part = lax.conv_general_dilated(
        grad_padded,
        spatial_kernel[::-1, ::-1],
        (1, 1),
        ((0, 0), (1, 1)),
        dimension_numbers=("NHCW", "HWOI", "NHCW"),
        preferred_element_type=jnp.float32,
    )
    kernel_terms = lax.conv_general_dilated(
        input_rows,
        grad_pre,
        (1, 1),
        ((0, 0), (1, 1)),
        dimension_numbers=("CHNW", "IHOW", "NHCW"),
        preferred_element_type=jnp.float32,
    )
    spatial_grad = factor * jnp.transpose(kernel_terms, (1, 3, 0, 2))
    input_full = input_part.astype(jnp.bfloat16)
    output, input_grad = (
        lax.all_to_all(output_full, "chan", split_axis=2, concat_axis=0, tiled=True),
        lax.all_to_all(input_full, "chan", split_axis=2, concat_axis=0, tiled=True),
    )
    spatial_total, temporal_total = lax.psum((spatial_grad, temporal_grad), ("tm", "axial", "chan"))
    mid_start = lax.axis_index("chan") * mid_share
    spatial_grad = lax.dynamic_slice_in_dim(spatial_total, mid_start, mid_share, 3)
    temporal_grad = lax.dynamic_slice_in_dim(temporal_total, mid_start, mid_share, 1)
    return (output, input_grad, spatial_grad, temporal_grad)


def solution(mesh):
    placed = (
        P(("parts", "tm"), "axial", None, None),
        P("parts", None, None, "chan"),
        P("parts", "chan", None),
        P(("parts", "tm"), "axial", None, None),
    )
    return jax.shard_map(
        shards,
        mesh=mesh,
        in_specs=placed,
        out_specs=(
            P(("parts", "tm"), "axial", "chan", None),
            P(("parts", "tm"), "axial", "chan", None),
            P("parts", None, None, "chan"),
            P("parts", "chan", None),
        ),
        check_vma=False,
    )
```

profile of v0, /device:TPU:0, one launch (start us, length us, event | category | flops | bytes accessed | tf_op | source)
XLA Modules:
  0.0 171.0 jit_solution(202611430970531133)
XLA Ops:
  7.3 0.9 constant_dynamic-slice_fusion.1
  8.2 4.9 %collective-permute-start = (bf16[3,1,64,128]{3,2,1,0:T(8,128)(2,1)S(1)}, bf16[3,1,64,128]{3,2,1,0:T(8,128)(2,1)S(1)}, u32[]{:S(2)}, u32[]{:S(2)}) collective-permute-start(bf16[3,1,64,128]{3,2,1,0:T(8,128)(2,1)S(1)} %get-tuple-element.15), channel_id=1, source_target_pairs={{0,2},{1,3},{4,6},{5,7},{8,10},{9,11},{12,14},{13,15},{16,18},{17,... | collective-permute-start | bytes 147464 | tf_op jit(solution)/shard_map/ppermute | solution.py:15
  13.0 1.3 collective-permute-start.1
  14.3 0.9 copy.76
  15.2 1.9 %all_gather.7 = bf16[3,144,64]{2,0,1:T(4,128)(2,1)S(1)} all-gather(bf16[3,72,64]{2,0,1:T(4,128)(2,1)S(1)} %copy.76), channel_id=1, replica_groups=mesh['parts'=2,'tm'=4,'axial'=2,'chan'=2] {'chan'}, dimensions={1}, use_global_device_ids=true | all-gather | bytes 82944 | tf_op jit(solution)/shard_map/all_gather | solution.py:56
  17.2 0.2 fusion.54
  17.3 0.1 copy.103
  17.5 1.2 fusion.42
  18.7 0.1 copy.101
  18.8 0.1 copy.104
  18.9 0.2 copy.72
  19.1 2.1 %all_gather.6 = bf16[3,3,64,144]{2,1,0,3:T(4,128)(2,1)S(1)} all-gather(bf16[3,3,64,72]{2,1,0,3:T(4,128)(2,1)S(1)} %copy.72), channel_id=1, replica_groups=mesh['parts'=2,'tm'=4,'axial'=2,'chan'=2] {'chan'}, dimensions={3}, use_global_device_ids=true | all-gather | bytes 248832 | tf_op jit(solution)/shard_map/all_gather | solution.py:55
  21.2 0.3 copy.73
  21.6 1.3 copy.93
  22.9 0.3 copy.107
  23.2 0.2 pad.clone
  23.4 0.2 reshape.10
  23.7 0.4 fusion.20
  24.1 2.6 %add_divide_fusion = (f32[4,24,17,144]{3,1,2,0:T(8,128)S(1)}, bf16[4,24,17,144]{3,1,2,0:T(8,128)(2,1)}, f32[4,24,17,144]{3,1,2,0:T(8,128)}) fusion(pred[24,17]{0,1:T(8,128)(4,1)S(1)} %copy-done.16, bf16[3,3,64,144]{3,2,1,0:T(8,128)(2,1)S(1)} %copy.73, bf16[6,64,3,8,19]{1,4,3,2,0:T(8,128)(2,1)S(1)} %fusion.20), kind=kOutput, calls=%fused_computation.7 | convolution fusion | flops 272844288 | bytes 2866584 | tf_op jit(solution)/shard_map/conv_general_dilated | solution.py:24
  26.7 0.6 copy.82
  27.4 0.3 slice.87
  27.7 1.0 copy.105
  28.6 1.5 copy.74
  30.1 1.2 slice.82
  31.3 1.5 copy.102
  32.8 0.9 convolution_bitcast_fusion.1
  33.7 0.8 pad_maximum_fusion.3
  34.5 0.2 collective-permute-start.2
  34.6 3.4 %collective-permute-start.3 = (bf16[1,4,208,128]{3,2,1,0:T(8,128)(2,1)}, bf16[1,4,208,128]{3,2,1,0:T(8,128)(2,1)}, u32[]{:S(2)}, u32[]{:S(2)}) collective-permute-start(bf16[1,4,208,128]{3,2,1,0:T(8,128)(2,1)} %get-tuple-element.12), channel_id=1, source_target_pairs={{1,0},{4,1},{5,4},{8,5},{9,8},{12,9},{13,12},{0,13},{3,2},{6,3},{7... | collective-permute-start | bytes 638984 | tf_op jit(solution)/shard_map/ppermute | solution.py:18
  38.0 0.6 copy.84
  38.7 0.3 slice.88
  39.0 1.5 copy.106
  40.5 1.7 fusion.44
  42.2 2.1 %maximum_maximum_fusion = (bf16[4,4,208,128]{3,2,1,0:T(8,128)(2,1)}, bf16[4,4,208,128]{3,2,1,0:T(8,128)(2,1)S(1)}) fusion(bf16[3,4,64,128]{3,2,1,0:T(8,128)(2,1)S(1)} %constant_dynamic-slice_fusion.4, bf16[3,4,144,128]{3,2,1,0:T(8,128)(2,1)S(1)} %bitcast.111, bf16[1,4,208,128]{3,2,1,0:T(8,128)(2,1)} %collective-permute-done.2, ...), kind=kLoop, calls=%fused_computation.28 | loop fusion | flops 5111808 | bytes 2768896 | tf_op jit(solution)/shard_map/concatenate | solution.py:19
  44.4 0.9 convolution_bitcast_fusion
  45.3 1.0 fusion.25
  46.2 1.1 fusion.29
  47.4 1.2 fusion.10
  48.7 1.4 copy.94
  50.1 0.3 convolution_bitcast_fusion.2
  50.4 0.2 fusion.19
  50.6 0.2 copy.80
  50.7 5.1 %all_to_all.36 = bf16[3,4,64,128]{3,1,0,2:T(4,128)(2,1)S(1)} all-to-all(bf16[3,4,64,128]{3,1,0,2:T(4,128)(2,1)S(1)} %copy.80), channel_id=1, replica_groups=mesh['parts'=2,'tm'=4,'axial'=2,'chan'=2] {'chan'}, dimensions={2} | all-to-all | bytes 393216 | tf_op jit(solution)/shard_map/all_to_all | solution.py:113
  55.9 0.7 copy.81
  56.6 4.5 %collective-permute-start.4 = (bf16[3,1,144,128]{3,2,1,0:T(8,128)(2,1)S(1)}, bf16[3,1,144,128]{3,2,1,0:T(8,128)(2,1)S(1)}, u32[]{:S(2)}, u32[]{:S(2)}) collective-permute-start(bf16[3,1,144,128]{3,2,1,0:T(8,128)(2,1)S(1)} %get-tuple-element.13), channel_id=1, source_target_pairs={{0,2},{1,3},{4,6},{5,7},{8,10},{9,11},{12,14},{13,15},{16,18},{17,... | collective-permute-start | bytes 331784 | tf_op jit(solution)/shard_map/ppermute | solution.py:15
  61.2 1.6 collective-permute-start.5
  62.8 3.4 %convolution_multiply_fusion = f32[3,3,64,144]{3,2,1,0:T(8,128)} fusion(bf16[3,6,64,128]{2,0,3,1:T(4,128)(2,1)S(1)} %copy-done.8, bf16[3,4,144,128]{2,0,3,1:T(4,128)(2,1)S(1)} %copy-done.7), kind=kOutput, calls=%fused_computation.19 | convolution fusion | flops 253559808 | bytes 1069056 | tf_op jit(solution)/shard_map/transpose | solution.py:110
  66.2 0.7 maximum_multiply_fusion
  67.0 1.1 collective-permute-done.5
  68.0 0.1 maximum_bitcast_fusion
  68.1 0.6 copy.108
  68.7 0.5 pad.2.clone
  69.2 0.5 reshape.17
  69.9 0.7 fusion.1
  70.5 0.3 copy-done.10
  70.8 2.1 %fusion.14 = bf16[4,24,17,64]{3,1,2,0:T(8,128)(2,1)S(1)} fusion(bf16[3,3,64,144]{3,2,1,0:T(8,128)(2,1)S(1)} %copy-done.10, bf16[6,144,3,8,19]{1,4,3,2,0:T(8,128)(2,1)S(1)} %fusion.1, pred[24,17]{0,1:T(8,128)(4,1)S(1)} %copy-done.17), kind=kOutput, calls=%fused_computation.18 | convolution fusion | flops 270938112 | bytes 1163160 | tf_op jit(solution)/shard_map/conv_general_dilated | solution.py:94
  72.9 0.2 copy.89
  73.1 0.1 slice_bitcast_fusion
  73.2 0.2 copy.90
  73.5 3.9 %all_to_all.37 = bf16[3,4,64,128]{3,1,0,2:T(4,128)(2,1)S(1)} all-to-all(bf16[3,4,64,128]{3,1,0,2:T(4,128)(2,1)S(1)} %copy.90), channel_id=1, replica_groups=mesh['parts'=2,'tm'=4,'axial'=2,'chan'=2] {'chan'}, dimensions={2} | all-to-all | bytes 393216 | tf_op jit(solution)/shard_map/all_to_all | solution.py:114
  77.4 0.7 copy.92
  78.1 82.5 %all-reduce.3.cloned.1.call-done = (f32[3,3,64,144]{3,2,1,0:T(8,128)}, f32[3,144,64]{1,2,0:T(8,128)}) async-done(((f32[3,3,64,144]{3,2,1,0:T(8,128)}, f32[3,144,64]{1,2,0:T(8,128)}), (f32[3,3,64,144]{3,2,1,0:T(8,128)}, f32[3,144,64]{1,2,0:T(8,128)})) %all-reduce.3.cloned.1.call-update) | async-done | bytes 442384 | tf_op jit(solution)/shard_map/psum | solution.py:116
  160.6 1.9 %constant_dynamic-slice_fusion.3 = f32[3,3,64,72]{3,2,1,0:T(8,128)} fusion(f32[3,3,64,144]{3,2,1,0:T(8,128)} %get-tuple-element.4, s32[]{:T(128)S(6)} %select_n.9), kind=kLoop, calls=%fused_computation.66 | loop fusion | bytes 331780 | tf_op jit(solution)/shard_map/dynamic_slice | solution.py:118
  162.5 1.7 constant_dynamic-slice_fusion.2
  (49 shorter events, 0.4 us)
Async XLA Ops:
  7.2 10.2 %copy-start = (bf16[6,4,64,128]{3,2,1,0:T(8,128)(2,1)S(1)}, bf16[6,4,64,128]{3,2,1,0:T(8,128)(2,1)}, u32[]{:S(2)}) copy-start(bf16[6,4,64,128]{3,2,1,0:T(8,128)(2,1)} %param.7) | copy-start | bytes 1179652
  7.2 11.5 %copy-start.13 = (bf16[6,4,64,128]{3,2,1,0:T(8,128)(2,1)S(1)}, bf16[6,4,64,128]{3,2,1,0:T(8,128)(2,1)}, u32[]{:S(2)}) copy-start(bf16[6,4,64,128]{3,2,1,0:T(8,128)(2,1)} %param.4) | copy-start | bytes 1179652
  7.2 11.7 %copy-start.14 = (bf16[3,3,64,72]{3,2,1,0:T(8,128)(2,1)S(1)}, bf16[3,3,64,72]{3,2,1,0:T(8,128)(2,1)}, u32[]{:S(2)}) copy-start(bf16[3,3,64,72]{3,2,1,0:T(8,128)(2,1)} %param.5) | copy-start | bytes 248836
  7.2 153.4 %all-reduce.3.cloned.1.call-start = ((), (), s32[]{:S(2)}) async-start(), calls=%async_computation.2 | async-start | bytes 1572864 | tf_op jit(solution)/shard_map/psum | solution.py:116
  8.2 13.4 %collective-permute-start = (bf16[3,1,64,128]{3,2,1,0:T(8,128)(2,1)S(1)}, bf16[3,1,64,128]{3,2,1,0:T(8,128)(2,1)S(1)}, u32[]{:S(2)}, u32[]{:S(2)}) collective-permute-start(bf16[3,1,64,128]{3,2,1,0:T(8,128)(2,1)S(1)} %get-tuple-element.15), channel_id=1, source_target_pairs={{0,2},{1,3},{4,6},{5,7},{8,10},{9,11},{12,14},{13,15},{16,18},{17,... | collective-permute-start | bytes 147464 | tf_op jit(solution)/shard_map/ppermute | solution.py:15
  13.0 8.5 %collective-permute-start.1 = (bf16[3,1,64,128]{3,2,1,0:T(8,128)(2,1)S(1)}, bf16[3,1,64,128]{3,2,1,0:T(8,128)(2,1)S(1)}, u32[]{:S(2)}, u32[]{:S(2)}) collective-permute-start(bf16[3,1,64,128]{3,2,1,0:T(8,128)(2,1)S(1)} %get-tuple-element.16), channel_id=1, source_target_pairs={{2,0},{3,1},{6,4},{7,5},{10,8},{11,9},{14,12},{15,13},{18,16},{19,... | collective-permute-start | bytes 147464 | tf_op jit(solution)/shard_map/ppermute | solution.py:18
  17.4 1.5 copy-start.11
  21.6 2.5 %copy-start.9 = (bf16[3,3,64,144]{3,2,1,0:T(8,128)(2,1)}, bf16[3,3,64,144]{3,2,1,0:T(8,128)(2,1)S(1)}, u32[]{:S(2)}) copy-start(bf16[3,3,64,144]{3,2,1,0:T(8,128)(2,1)S(1)} %copy.73) | copy-start | bytes 497668
  23.4 0.7 copy-start.16
  32.8 5.3 %copy-start.4 = (f32[4,24,17,144]{3,1,2,0:T(8,128)S(1)}, f32[4,24,17,144]{3,1,2,0:T(8,128)}, u32[]{:S(2)}) copy-start(f32[4,24,17,144]{3,1,2,0:T(8,128)} %get-tuple-element.8) | copy-start | bytes 2820100
  34.5 7.7 %collective-permute-start.2 = (bf16[1,4,208,128]{3,2,1,0:T(8,128)(2,1)}, bf16[1,4,208,128]{3,2,1,0:T(8,128)(2,1)}, u32[]{:S(2)}, u32[]{:S(2)}) collective-permute-start(bf16[1,4,208,128]{3,2,1,0:T(8,128)(2,1)} %get-tuple-element.11), channel_id=1, source_target_pairs={{0,1},{1,4},{4,5},{5,8},{8,9},{9,12},{12,13},{13,0},{2,3},{3,6},{6... | collective-permute-start | bytes 638984 | tf_op jit(solution)/shard_map/ppermute | solution.py:15
  34.6 7.6 %collective-permute-start.3 = (bf16[1,4,208,128]{3,2,1,0:T(8,128)(2,1)}, bf16[1,4,208,128]{3,2,1,0:T(8,128)(2,1)}, u32[]{:S(2)}, u32[]{:S(2)}) collective-permute-start(bf16[1,4,208,128]{3,2,1,0:T(8,128)(2,1)} %get-tuple-element.12), channel_id=1, source_target_pairs={{1,0},{4,1},{5,4},{8,5},{9,8},{12,9},{13,12},{0,13},{3,2},{6,3},{7... | collective-permute-start | bytes 638984 | tf_op jit(solution)/shard_map/ppermute | solution.py:18
  44.4 3.0 %copy-start.1 = (f32[4,3,128,144]{2,3,0,1:T(8,128)S(1)}, f32[4,3,128,144]{2,3,0,1:T(8,128)}, u32[]{:S(2)}) copy-start(f32[4,3,128,144]{2,3,0,1:T(8,128)} %copy.106) | copy-start | bytes 2654212
  44.4 3.0 %copy-start.2 = (f32[3,4,128,144]{2,3,1,0:T(8,128)S(1)}, f32[3,4,128,144]{2,3,1,0:T(8,128)}, u32[]{:S(2)}) copy-start(f32[3,4,128,144]{2,3,1,0:T(8,128)} %fusion.42) | copy-start | bytes 2654212
  48.6 1.5 copy-start.3
  48.6 1.7 %copy-start.5 = (f32[3,4,128,64]{2,3,1,0:T(8,128)S(1)}, f32[3,4,128,64]{2,3,1,0:T(8,128)}, u32[]{:S(2)}) copy-start(f32[3,4,128,64]{2,3,1,0:T(8,128)} %fusion.44) | copy-start | bytes 1179652
  48.6 1.7 %copy-start.6 = (f32[3,4,128,64]{2,3,1,0:T(8,128)S(1)}, f32[3,4,128,64]{2,3,1,0:T(8,128)}, u32[]{:S(2)}) copy-start(f32[3,4,128,64]{2,3,1,0:T(8,128)} %fusion.25) | copy-start | bytes 1179652
  50.1 12.7 %copy-start.7 = (bf16[3,4,144,128]{2,0,3,1:T(4,128)(2,1)S(1)}, bf16[3,4,144,128]{2,0,3,1:T(4,128)(2,1)}, u32[]{:S(2)}) copy-start(bf16[3,4,144,128]{2,0,3,1:T(4,128)(2,1)} %copy.94) | copy-start | bytes 1327108
  50.1 12.7 %copy-start.8 = (bf16[3,6,64,128]{2,0,3,1:T(4,128)(2,1)S(1)}, bf16[3,6,64,128]{2,0,3,1:T(4,128)(2,1)}, u32[]{:S(2)}) copy-start(bf16[3,6,64,128]{2,0,3,1:T(4,128)(2,1)} %copy.93) | copy-start | bytes 884740
  56.6 10.4 %collective-permute-start.4 = (bf16[3,1,144,128]{3,2,1,0:T(8,128)(2,1)S(1)}, bf16[3,1,144,128]{3,2,1,0:T(8,128)(2,1)S(1)}, u32[]{:S(2)}, u32[]{:S(2)}) collective-permute-start(bf16[3,1,144,128]{3,2,1,0:T(8,128)(2,1)S(1)} %get-tuple-element.13), channel_id=1, source_target_pairs={{0,2},{1,3},{4,6},{5,7},{8,10},{9,11},{12,14},{13,15},{16,18},{17,... | collective-permute-start | bytes 331784 | tf_op jit(solution)/shard_map/ppermute | solution.py:15
  61.1 5.1 %copy-start.12 = (f32[1,144,64]{1,2,0:T(8,128)S(1)}, f32[1,144,64]{1,2,0:T(8,128)}, u32[]{:S(2)}) copy-start(f32[1,144,64]{1,2,0:T(8,128)} %convolution_bitcast_fusion.1) | copy-start | bytes 110596
  61.2 5.1 %copy-start.15 = (f32[1,144,64]{1,2,0:T(8,128)S(1)}, f32[1,144,64]{1,2,0:T(8,128)}, u32[]{:S(2)}) copy-start(f32[1,144,64]{1,2,0:T(8,128)} %convolution_bitcast_fusion) | copy-start | bytes 110596
  61.2 6.9 %collective-permute-start.5 = (bf16[3,1,144,128]{3,2,1,0:T(8,128)(2,1)S(1)}, bf16[3,1,144,128]{3,2,1,0:T(8,128)(2,1)S(1)}, u32[]{:S(2)}, u32[]{:S(2)}) collective-permute-start(bf16[3,1,144,128]{3,2,1,0:T(8,128)(2,1)S(1)} %get-tuple-element.14), channel_id=1, source_target_pairs={{2,0},{3,1},{6,4},{7,5},{10,8},{11,9},{14,12},{15,13},{18,16},{19,... | collective-permute-start | bytes 331784 | tf_op jit(solution)/shard_map/ppermute | solution.py:18
  69.9 1.0 copy-start.10
  69.9 1.0 copy-start.17
Sparse Core Ops, SparseCore 0:
  67.1 93.4 all-reduce.2
where the time goes:
time: 172 us; the launch traced here: 171 us
  waiting for transfers between devices  83.6 us (49%)
  local copies, waits for them, and re-layouts  22.5 us (13%)
  matrix products  16.7 us (10%)
  starting transfers between devices  15.9 us (9%)
  between operations  14.6 us (8%)
  blocking collectives  13.1 us (8%)
  other arithmetic  4.78 us (3%)
    psum x1, waiting for transfers between devices, shards(): lax.psum((spatial_grad, temporal_grad), ('tm', 'axial', 'chan'))  82.5 us
    ppermute x3, starting transfers between devices, extended_2(): lax.ppermute(lax.slice_in_dim(block, block.shape[dim] - width, None, axis...  9.55 us
    unnamed x46, local copies, waits for them, and re-layouts  6.65 us
    ppermute x3, starting transfers between devices, extended_2(): lax.ppermute(lax.slice_in_dim(block, 0, width, axis=dim), axis, backward)  6.29 us
    all_to_all x1, blocking collectives, shards(): lax.all_to_all(output_full, 'chan', split_axis=2, concat_axis=0, tiled=True)  5.14 us
    all_to_all x1, blocking collectives, shards(): lax.all_to_all(input_full, 'chan', split_axis=2, concat_axis=0, tiled=True)  3.89 us
    dot_general x3, matrix products, shards(): jnp.einsum('fhcw,mc->fhmw', upstream_wide[2 - offset:2 - offset + frame_l...  3.59 us
  transfers between devices with their start and end apart: 7, of which 2 were waited for; matrix products, arithmetic and copies ran while one was open for 10% of the time, Pallas kernels for 0%

commit v1 on v0

--- a/solution.py
+++ b/solution.py
@@ -113,7 +113,9 @@
         lax.all_to_all(output_full, "chan", split_axis=2, concat_axis=0, tiled=True),
         lax.all_to_all(input_full, "chan", split_axis=2, concat_axis=0, tiled=True),
     )
-    spatial_total, temporal_total = lax.psum((spatial_grad, temporal_grad), ("tm", "axial", "chan"))
+    spatial_total, temporal_total = lax.psum(
+        lax.psum((spatial_grad, temporal_grad), ("axial", "chan")), "tm"
+    )
     mid_start = lax.axis_index("chan") * mid_share
     spatial_grad = lax.dynamic_slice_in_dim(spatial_total, mid_start, mid_share, 3)
     temporal_grad = lax.dynamic_slice_in_dim(temporal_total, mid_start, mid_share, 1)

time: 172 us -> 160 us (0.930)
  waiting for transfers between devices: 83.6 us -> 69.6 us
    psum x1 -> x2, waiting for transfers between devices: 82.5 us -> 68.5 us  [the longest x1 37.5 us: shards(): lax.psum(lax.psum((spatial_grad, temporal_grad), ('axial', 'chan')), 'tm')]
  transfers between devices with their start and end apart: 7 -> 8, of which waited for: 2 -> 3; matrix products, arithmetic and copies ran while one was open for 10% -> 12% of each run, Pallas kernels for 0% -> 0%
where the time goes in v1:
time: 160 us
  waiting for transfers between devices  69.6 us (43%)
  local copies, waits for them, and re-layouts  22.2 us (14%)
  matrix products  18.1 us (11%)
  starting transfers between devices  15.9 us (10%)
  between operations  14.6 us (9%)
  blocking collectives  13.1 us (8%)
  other arithmetic  6.01 us (4%)
    psum x1, waiting for transfers between devices, shards(): lax.psum(lax.psum((spatial_grad, temporal_grad), ('axial', 'chan')), 'tm')  37.5 us
    psum x1, waiting for transfers between devices, shards(): lax.psum((spatial_grad, temporal_grad), ('axial', 'chan'))  31 us
    ppermute x3, starting transfers between devices, extended_2(): lax.ppermute(lax.slice_in_dim(block, block.shape[dim] - width, None, axis...  9.56 us
    unnamed x46, local copies, waits for them, and re-layouts  6.38 us
    ppermute x3, starting transfers between devices, extended_2(): lax.ppermute(lax.slice_in_dim(block, 0, width, axis=dim), axis, backward)  6.28 us
    all_to_all x1, blocking collectives, shards(): lax.all_to_all(output_full, 'chan', split_axis=2, concat_axis=0, tiled=True)  5.13 us
    all_to_all x1, blocking collectives, shards(): lax.all_to_all(input_full, 'chan', split_axis=2, concat_axis=0, tiled=True)  3.89 us
    dot_general x3, matrix products, shards(): jnp.einsum('fhcw,mc->fhmw', upstream_wide[2 - offset:2 - offset + frame_l...  3.59 us
  transfers between devices with their start and end apart: 8, of which 3 were waited for; matrix products, arithmetic and copies ran while one was open for 12% of the time, Pallas kernels for 0%

profile of v1, /device:TPU:0, one launch (start us, length us, event | category | flops | bytes accessed | tf_op | source)
XLA Modules:
  0.0 159.5 jit_solution(17464763433525423335)
XLA Ops:
  7.3 0.9 constant_dynamic-slice_fusion.1
  8.2 4.9 %collective-permute-start = (bf16[3,1,64,128]{3,2,1,0:T(8,128)(2,1)S(1)}, bf16[3,1,64,128]{3,2,1,0:T(8,128)(2,1)S(1)}, u32[]{:S(2)}, u32[]{:S(2)}) collective-permute-start(bf16[3,1,64,128]{3,2,1,0:T(8,128)(2,1)S(1)} %get-tuple-element.17), channel_id=1, source_target_pairs={{0,2},{1,3},{4,6},{5,7},{8,10},{9,11},{12,14},{13,15},{16,18},{17,... | collective-permute-start | bytes 147464 | tf_op jit(solution)/shard_map/ppermute | solution.py:15
  13.0 1.3 collective-permute-start.1
  14.3 0.9 copy.76
  15.2 1.9 %all_gather.7 = bf16[3,144,64]{2,0,1:T(4,128)(2,1)S(1)} all-gather(bf16[3,72,64]{2,0,1:T(4,128)(2,1)S(1)} %copy.76), channel_id=1, replica_groups=mesh['parts'=2,'tm'=4,'axial'=2,'chan'=2] {'chan'}, dimensions={1}, use_global_device_ids=true | all-gather | bytes 82944 | tf_op jit(solution)/shard_map/all_gather | solution.py:56
  17.2 0.2 fusion.54
  17.3 0.1 copy.103
  17.5 1.2 fusion.42
  18.7 0.1 copy.101
  18.8 0.1 copy.104
  18.9 0.2 copy.72
  19.1 2.1 %all_gather.6 = bf16[3,3,64,144]{2,1,0,3:T(4,128)(2,1)S(1)} all-gather(bf16[3,3,64,72]{2,1,0,3:T(4,128)(2,1)S(1)} %copy.72), channel_id=1, replica_groups=mesh['parts'=2,'tm'=4,'axial'=2,'chan'=2] {'chan'}, dimensions={3}, use_global_device_ids=true | all-gather | bytes 248832 | tf_op jit(solution)/shard_map/all_gather | solution.py:55
  21.2 0.3 copy.73
  21.6 1.3 copy.93
  22.9 0.3 copy.107
  23.2 0.2 pad.clone
  23.5 0.2 reshape.10
  23.7 0.4 fusion.20
  24.1 2.6 %add_divide_fusion = (f32[4,24,17,144]{3,1,2,0:T(8,128)S(1)}, bf16[4,24,17,144]{3,1,2,0:T(8,128)(2,1)}, f32[4,24,17,144]{3,1,2,0:T(8,128)}) fusion(pred[24,17]{0,1:T(8,128)(4,1)S(1)} %copy-done.16, bf16[3,3,64,144]{3,2,1,0:T(8,128)(2,1)S(1)} %copy.73, bf16[6,64,3,8,19]{1,4,3,2,0:T(8,128)(2,1)S(1)} %fusion.20), kind=kOutput, calls=%fused_computation.7 | convolution fusion | flops 272844288 | bytes 2866584 | tf_op jit(solution)/shard_map/conv_general_dilated | solution.py:24
  26.7 0.6 copy.82
  27.4 0.3 slice.87
  27.7 1.0 copy.105
  28.6 1.5 copy.74
  30.1 1.2 slice.82
  31.3 1.5 copy.102
  32.8 0.9 convolution_bitcast_fusion.1
  33.7 0.8 pad_maximum_fusion.3
  34.5 0.2 collective-permute-start.2
  34.6 3.4 %collective-permute-start.3 = (bf16[1,4,208,128]{3,2,1,0:T(8,128)(2,1)}, bf16[1,4,208,128]{3,2,1,0:T(8,128)(2,1)}, u32[]{:S(2)}, u32[]{:S(2)}) collective-permute-start(bf16[1,4,208,128]{3,2,1,0:T(8,128)(2,1)} %get-tuple-element.14), channel_id=1, source_target_pairs={{1,0},{4,1},{5,4},{8,5},{9,8},{12,9},{13,12},{0,13},{3,2},{6,3},{7... | collective-permute-start | bytes 638984 | tf_op jit(solution)/shard_map/ppermute | solution.py:18
  38.0 0.6 copy.84
  38.7 0.3 slice.88
  39.0 1.6 copy.106
  40.5 1.7 %fusion.44 = f32[3,4,128,64]{2,3,1,0:T(8,128)} fusion(bf16[1,144,64]{1,2,0:T(8,128)(2,1)} %copy-done.11, bf16[4,3,128,144]{2,3,0,1:T(8,128)(2,1)S(1)} %copy.102), kind=kOutput, calls=%fused_computation.59 | convolution fusion | flops 28311552 | bytes 854016 | tf_op jit(solution)/shard_map/fhmw,mc->fhcw/dot_general | solution.py:38
  42.2 2.1 %maximum_maximum_fusion = (bf16[4,4,208,128]{3,2,1,0:T(8,128)(2,1)}, bf16[4,4,208,128]{3,2,1,0:T(8,128)(2,1)S(1)}) fusion(bf16[3,4,64,128]{3,2,1,0:T(8,128)(2,1)S(1)} %constant_dynamic-slice_fusion.4, bf16[3,4,144,128]{3,2,1,0:T(8,128)(2,1)S(1)} %bitcast.111, bf16[1,4,208,128]{3,2,1,0:T(8,128)(2,1)} %collective-permute-done.2, ...), kind=kLoop, calls=%fused_computation.28 | loop fusion | flops 5111808 | bytes 2768896 | tf_op jit(solution)/shard_map/concatenate | solution.py:19
  44.4 0.9 convolution_bitcast_fusion
  45.3 1.0 fusion.25
  46.2 1.1 fusion.29
  47.4 1.2 fusion.10
  48.7 1.4 copy.94
  50.1 0.3 convolution_bitcast_fusion.2
  50.4 0.2 fusion.19
  50.6 0.2 copy.80
  50.7 5.1 %all_to_all.36 = bf16[3,4,64,128]{3,1,0,2:T(4,128)(2,1)S(1)} all-to-all(bf16[3,4,64,128]{3,1,0,2:T(4,128)(2,1)S(1)} %copy.80), channel_id=1, replica_groups=mesh['parts'=2,'tm'=4,'axial'=2,'chan'=2] {'chan'}, dimensions={2} | all-to-all | bytes 393216 | tf_op jit(solution)/shard_map/all_to_all | solution.py:113
  55.9 0.7 copy.81
  56.6 4.5 %collective-permute-start.4 = (bf16[3,1,144,128]{3,2,1,0:T(8,128)(2,1)S(1)}, bf16[3,1,144,128]{3,2,1,0:T(8,128)(2,1)S(1)}, u32[]{:S(2)}, u32[]{:S(2)}) collective-permute-start(bf16[3,1,144,128]{3,2,1,0:T(8,128)(2,1)S(1)} %get-tuple-element.15), channel_id=1, source_target_pairs={{0,2},{1,3},{4,6},{5,7},{8,10},{9,11},{12,14},{13,15},{16,18},{17,... | collective-permute-start | bytes 331784 | tf_op jit(solution)/shard_map/ppermute | solution.py:15
  61.2 1.6 %collective-permute-start.5 = (bf16[3,1,144,128]{3,2,1,0:T(8,128)(2,1)S(1)}, bf16[3,1,144,128]{3,2,1,0:T(8,128)(2,1)S(1)}, u32[]{:S(2)}, u32[]{:S(2)}) collective-permute-start(bf16[3,1,144,128]{3,2,1,0:T(8,128)(2,1)S(1)} %get-tuple-element.16), channel_id=1, source_target_pairs={{2,0},{3,1},{6,4},{7,5},{10,8},{11,9},{14,12},{15,13},{18,16},{19,... | collective-permute-start | bytes 331784 | tf_op jit(solution)/shard_map/ppermute | solution.py:18
  62.8 3.4 %convolution_multiply_fusion = f32[3,3,64,144]{3,2,1,0:T(8,128)} fusion(bf16[3,6,64,128]{2,0,3,1:T(4,128)(2,1)S(1)} %copy-done.8, bf16[3,4,144,128]{2,0,3,1:T(4,128)(2,1)S(1)} %copy-done.7), kind=kOutput, calls=%fused_computation.19 | convolution fusion | flops 253559808 | bytes 1069056 | tf_op jit(solution)/shard_map/transpose | solution.py:110
  66.2 0.7 maximum_multiply_fusion
  67.0 1.0 collective-permute-done.5
  68.0 0.1 maximum_bitcast_fusion
  68.1 0.6 copy.108
  68.7 0.5 pad.2.clone
  69.2 0.5 reshape.17
  69.9 1.9 %fusion.1 = bf16[6,144,3,8,19]{1,4,3,2,0:T(8,128)(2,1)} fusion(bf16[6,144,3,7,2]{1,4,3,2,0:T(2,128)(2,1)S(1)} %slice.91, bf16[6,144,3,8,17]{1,4,3,2,0:T(8,128)(2,1)S(1)} %reshape.17), kind=kLoop, calls=%fused_computation.2 | loop fusion | flops 2363904 | bytes 1565568 | tf_op jit(solution)/shard_map/conv_general_dilated | solution.py:94
  71.8 31.0 %all-reduce.5.cloned.1.call-done = (f32[3,3,64,144]{3,2,1,0:T(8,128)}, f32[3,144,64]{1,2,0:T(8,128)}) async-done(((f32[3,3,64,144]{3,2,1,0:T(8,128)}, f32[3,144,64]{1,2,0:T(8,128)}), (f32[3,3,64,144]{3,2,1,0:T(8,128)}, f32[3,144,64]{1,2,0:T(8,128)})) %all-reduce.5.cloned.1.call-update) | async-done | bytes 442384 | tf_op jit(solution)/shard_map/psum | solution.py:117
  102.8 3.6 %fusion.14 = bf16[4,24,17,64]{3,1,2,0:T(8,128)(2,1)S(1)} fusion(bf16[3,3,64,144]{3,2,1,0:T(8,128)(2,1)S(1)} %copy-done.10, bf16[6,144,3,8,19]{1,4,3,2,0:T(8,128)(2,1)} %fusion.1, pred[24,17]{0,1:T(8,128)(4,1)S(1)} %copy-done.17), kind=kOutput, calls=%fused_computation.18 | convolution fusion | flops 270938112 | bytes 1163160 | tf_op jit(solution)/shard_map/conv_general_dilated | solution.py:94
  106.4 0.2 copy.89
  106.6 0.1 slice_bitcast_fusion
  106.7 0.2 copy.90
  106.9 3.9 %all_to_all.37 = bf16[3,4,64,128]{3,1,0,2:T(4,128)(2,1)S(1)} all-to-all(bf16[3,4,64,128]{3,1,0,2:T(4,128)(2,1)S(1)} %copy.90), channel_id=1, replica_groups=mesh['parts'=2,'tm'=4,'axial'=2,'chan'=2] {'chan'}, dimensions={2} | all-to-all | bytes 393216 | tf_op jit(solution)/shard_map/all_to_all | solution.py:114
  110.9 0.7 copy.92
  111.6 37.5 %all-reduce.7.cloned.1.call-done = (f32[3,3,64,144]{3,2,1,0:T(8,128)}, f32[3,144,64]{1,2,0:T(8,128)}) async-done(((f32[3,3,64,144]{3,2,1,0:T(8,128)}, f32[3,144,64]{1,2,0:T(8,128)}), (f32[3,3,64,144]{3,2,1,0:T(8,128)}, f32[3,144,64]{1,2,0:T(8,128)})) %all-reduce.7.cloned.1.call-update) | async-done | bytes 442384 | tf_op jit(solution)/shard_map/psum | solution.py:116
  149.1 1.9 %constant_dynamic-slice_fusion.3 = f32[3,3,64,72]{3,2,1,0:T(8,128)} fusion(f32[3,3,64,144]{3,2,1,0:T(8,128)} %get-tuple-element.6, s32[]{:T(128)S(6)} %select_n.9), kind=kLoop, calls=%fused_computation.66 | loop fusion | bytes 331780 | tf_op jit(solution)/shard_map/dynamic_slice | solution.py:120
  151.0 1.7 %constant_dynamic-slice_fusion.2 = f32[3,72,64]{1,2,0:T(8,128)} fusion(f32[3,144,64]{1,2,0:T(8,128)} %get-tuple-element.7, s32[]{:T(128)S(6)} %select_n.9), kind=kLoop, calls=%fused_computation.65 | loop fusion | bytes 110596 | tf_op jit(solution)/shard_map/dynamic_slice | solution.py:121
  (52 shorter events, 0.5 us)
Async XLA Ops:
  7.2 10.2 %copy-start = (bf16[6,4,64,128]{3,2,1,0:T(8,128)(2,1)S(1)}, bf16[6,4,64,128]{3,2,1,0:T(8,128)(2,1)}, u32[]{:S(2)}) copy-start(bf16[6,4,64,128]{3,2,1,0:T(8,128)(2,1)} %param.7) | copy-start | bytes 1179652
  7.2 11.5 %copy-start.13 = (bf16[6,4,64,128]{3,2,1,0:T(8,128)(2,1)S(1)}, bf16[6,4,64,128]{3,2,1,0:T(8,128)(2,1)}, u32[]{:S(2)}) copy-start(bf16[6,4,64,128]{3,2,1,0:T(8,128)(2,1)} %param.4) | copy-start | bytes 1179652
  7.2 11.7 %copy-start.14 = (bf16[3,3,64,72]{3,2,1,0:T(8,128)(2,1)S(1)}, bf16[3,3,64,72]{3,2,1,0:T(8,128)(2,1)}, u32[]{:S(2)}) copy-start(bf16[3,3,64,72]{3,2,1,0:T(8,128)(2,1)} %param.5) | copy-start | bytes 248836
  7.2 95.6 %all-reduce.5.cloned.1.call-start = ((), (), s32[]{:S(2)}) async-start(), calls=%async_computation.2 | async-start | bytes 1572864 | tf_op jit(solution)/shard_map/psum | solution.py:117
  8.2 13.4 %collective-permute-start = (bf16[3,1,64,128]{3,2,1,0:T(8,128)(2,1)S(1)}, bf16[3,1,64,128]{3,2,1,0:T(8,128)(2,1)S(1)}, u32[]{:S(2)}, u32[]{:S(2)}) collective-permute-start(bf16[3,1,64,128]{3,2,1,0:T(8,128)(2,1)S(1)} %get-tuple-element.17), channel_id=1, source_target_pairs={{0,2},{1,3},{4,6},{5,7},{8,10},{9,11},{12,14},{13,15},{16,18},{17,... | collective-permute-start | bytes 147464 | tf_op jit(solution)/shard_map/ppermute | solution.py:15
  13.0 8.6 %collective-permute-start.1 = (bf16[3,1,64,128]{3,2,1,0:T(8,128)(2,1)S(1)}, bf16[3,1,64,128]{3,2,1,0:T(8,128)(2,1)S(1)}, u32[]{:S(2)}, u32[]{:S(2)}) collective-permute-start(bf16[3,1,64,128]{3,2,1,0:T(8,128)(2,1)S(1)} %get-tuple-element.18), channel_id=1, source_target_pairs={{2,0},{3,1},{6,4},{7,5},{10,8},{11,9},{14,12},{15,13},{18,16},{19,... | collective-permute-start | bytes 147464 | tf_op jit(solution)/shard_map/ppermute | solution.py:18
  17.4 1.5 copy-start.11
  21.6 2.5 %copy-start.9 = (bf16[3,3,64,144]{3,2,1,0:T(8,128)(2,1)}, bf16[3,3,64,144]{3,2,1,0:T(8,128)(2,1)S(1)}, u32[]{:S(2)}) copy-start(bf16[3,3,64,144]{3,2,1,0:T(8,128)(2,1)S(1)} %copy.73) | copy-start | bytes 497668
  23.4 0.7 copy-start.16
  32.8 5.3 %copy-start.4 = (f32[4,24,17,144]{3,1,2,0:T(8,128)S(1)}, f32[4,24,17,144]{3,1,2,0:T(8,128)}, u32[]{:S(2)}) copy-start(f32[4,24,17,144]{3,1,2,0:T(8,128)} %get-tuple-element.10) | copy-start | bytes 2820100
  34.5 7.7 %collective-permute-start.2 = (bf16[1,4,208,128]{3,2,1,0:T(8,128)(2,1)}, bf16[1,4,208,128]{3,2,1,0:T(8,128)(2,1)}, u32[]{:S(2)}, u32[]{:S(2)}) collective-permute-start(bf16[1,4,208,128]{3,2,1,0:T(8,128)(2,1)} %get-tuple-element.13), channel_id=1, source_target_pairs={{0,1},{1,4},{4,5},{5,8},{8,9},{9,12},{12,13},{13,0},{2,3},{3,6},{6... | collective-permute-start | bytes 638984 | tf_op jit(solution)/shard_map/ppermute | solution.py:15
  34.6 7.6 %collective-permute-start.3 = (bf16[1,4,208,128]{3,2,1,0:T(8,128)(2,1)}, bf16[1,4,208,128]{3,2,1,0:T(8,128)(2,1)}, u32[]{:S(2)}, u32[]{:S(2)}) collective-permute-start(bf16[1,4,208,128]{3,2,1,0:T(8,128)(2,1)} %get-tuple-element.14), channel_id=1, source_target_pairs={{1,0},{4,1},{5,4},{8,5},{9,8},{12,9},{13,12},{0,13},{3,2},{6,3},{7... | collective-permute-start | bytes 638984 | tf_op jit(solution)/shard_map/ppermute | solution.py:18
  44.4 3.0 %copy-start.1 = (f32[4,3,128,144]{2,3,0,1:T(8,128)S(1)}, f32[4,3,128,144]{2,3,0,1:T(8,128)}, u32[]{:S(2)}) copy-start(f32[4,3,128,144]{2,3,0,1:T(8,128)} %copy.106) | copy-start | bytes 2654212
  44.4 3.0 %copy-start.2 = (f32[3,4,128,144]{2,3,1,0:T(8,128)S(1)}, f32[3,4,128,144]{2,3,1,0:T(8,128)}, u32[]{:S(2)}) copy-start(f32[3,4,128,144]{2,3,1,0:T(8,128)} %fusion.42) | copy-start | bytes 2654212
  48.6 1.5 copy-start.3
  48.6 1.7 %copy-start.5 = (f32[3,4,128,64]{2,3,1,0:T(8,128)S(1)}, f32[3,4,128,64]{2,3,1,0:T(8,128)}, u32[]{:S(2)}) copy-start(f32[3,4,128,64]{2,3,1,0:T(8,128)} %fusion.44) | copy-start | bytes 1179652
  48.6 1.7 %copy-start.6 = (f32[3,4,128,64]{2,3,1,0:T(8,128)S(1)}, f32[3,4,128,64]{2,3,1,0:T(8,128)}, u32[]{:S(2)}) copy-start(f32[3,4,128,64]{2,3,1,0:T(8,128)} %fusion.25) | copy-start | bytes 1179652
  50.1 12.7 %copy-start.7 = (bf16[3,4,144,128]{2,0,3,1:T(4,128)(2,1)S(1)}, bf16[3,4,144,128]{2,0,3,1:T(4,128)(2,1)}, u32[]{:S(2)}) copy-start(bf16[3,4,144,128]{2,0,3,1:T(4,128)(2,1)} %copy.94) | copy-start | bytes 1327108
  50.1 12.7 %copy-start.8 = (bf16[3,6,64,128]{2,0,3,1:T(4,128)(2,1)S(1)}, bf16[3,6,64,128]{2,0,3,1:T(4,128)(2,1)}, u32[]{:S(2)}) copy-start(bf16[3,6,64,128]{2,0,3,1:T(4,128)(2,1)} %copy.93) | copy-start | bytes 884740
  56.6 10.4 %collective-permute-start.4 = (bf16[3,1,144,128]{3,2,1,0:T(8,128)(2,1)S(1)}, bf16[3,1,144,128]{3,2,1,0:T(8,128)(2,1)S(1)}, u32[]{:S(2)}, u32[]{:S(2)}) collective-permute-start(bf16[3,1,144,128]{3,2,1,0:T(8,128)(2,1)S(1)} %get-tuple-element.15), channel_id=1, source_target_pairs={{0,2},{1,3},{4,6},{5,7},{8,10},{9,11},{12,14},{13,15},{16,18},{17,... | collective-permute-start | bytes 331784 | tf_op jit(solution)/shard_map/ppermute | solution.py:15
  61.1 5.1 %copy-start.12 = (f32[1,144,64]{1,2,0:T(8,128)S(1)}, f32[1,144,64]{1,2,0:T(8,128)}, u32[]{:S(2)}) copy-start(f32[1,144,64]{1,2,0:T(8,128)} %convolution_bitcast_fusion.1) | copy-start | bytes 110596
  61.1 5.1 %copy-start.15 = (f32[1,144,64]{1,2,0:T(8,128)S(1)}, f32[1,144,64]{1,2,0:T(8,128)}, u32[]{:S(2)}) copy-start(f32[1,144,64]{1,2,0:T(8,128)} %convolution_bitcast_fusion) | copy-start | bytes 110596
  61.2 6.9 %collective-permute-start.5 = (bf16[3,1,144,128]{3,2,1,0:T(8,128)(2,1)S(1)}, bf16[3,1,144,128]{3,2,1,0:T(8,128)(2,1)S(1)}, u32[]{:S(2)}, u32[]{:S(2)}) collective-permute-start(bf16[3,1,144,128]{3,2,1,0:T(8,128)(2,1)S(1)} %get-tuple-element.16), channel_id=1, source_target_pairs={{2,0},{3,1},{6,4},{7,5},{10,8},{11,9},{14,12},{15,13},{18,16},{19,... | collective-permute-start | bytes 331784 | tf_op jit(solution)/shard_map/ppermute | solution.py:18
  66.9 82.2 %all-reduce.7.cloned.1.call-start = ((), (), s32[]{:S(2)}) async-start(), calls=%async_computation.3 | async-start | bytes 1572864 | tf_op jit(solution)/shard_map/psum | solution.py:116
  69.9 32.9 %copy-start.10 = (bf16[3,3,64,144]{3,2,1,0:T(8,128)(2,1)S(1)}, bf16[3,3,64,144]{3,2,1,0:T(8,128)(2,1)}, u32[]{:S(2)}) copy-start(bf16[3,3,64,144]{3,2,1,0:T(8,128)(2,1)} %copy-done.9) | copy-start | bytes 497668
  69.9 32.9 %copy-start.17 = (pred[24,17]{0,1:T(8,128)(4,1)S(1)}, pred[24,17]{0,1:T(8,128)(4,1)}, u32[]{:S(2)}) copy-start(pred[24,17]{0,1:T(8,128)(4,1)} %constant.33) | copy-start | bytes 1228
Sparse Core Ops, SparseCore 0:
  67.0 35.6 all-reduce.4
  105.2 43.8 all-reduce.6
